TPU v7x, 32 devices: a whole 2x2x4 slice. The times are simulated.
32 devices in a mesh: wide: 8 (over y, x, core), narrow: 4 (over z).
Axes of the slice: x: 2, y: 2, z: 4, core: 2. Of those that a mesh axis runs over, the one named last changes fastest.
Arguments:
- hidden_in: bfloat16 [4096, 1536], P('wide'), may hold values from -64 to 64
- segment_ids: int32 [4096], P('wide'), may hold values from 0 to 7, as said below
- seg_lengths: int32 [8], replicated, may hold values from 1 to 2048, as said below
- seg_offsets: int32 [8], replicated, may hold values from 0 to 4095, as said below
- block_table: int32 [8, 16], replicated, may hold values from -1 to 39, as said below
- attn_gain: bfloat16 [1536], replicated, may hold values from 0.099609375 to 1.8984375
- w_query: bfloat16 [1536, 1536], P('wide', 'narrow'), may hold values from -0.15625 to 0.15625
- b_query: bfloat16 [1536], P('narrow'), may hold values from -128 to 128
- w_keyval: bfloat16 [1536, 512], P('wide'), may hold values from -0.15625 to 0.15625
- b_keyval: bfloat16 [512], replicated, may hold values from -128 to 128
- w_out: bfloat16 [1536, 1536], P('narrow', 'wide'), may hold values from -0.15625 to 0.15625
- mlp_gain: bfloat16 [1536], replicated, may hold values from 0.099609375 to 1.8984375
- w_gate: bfloat16 [1536, 8960], P('wide', 'narrow'), may hold values from -0.15625 to 0.15625
- w_up: bfloat16 [1536, 8960], P('wide', 'narrow'), may hold values from -0.15625 to 0.15625
- w_down: bfloat16 [8960, 1536], P('narrow', 'wide'), may hold values from -0.0625 to 0.0625
- next_gain: bfloat16 [1536], replicated, may hold values from 0.099609375 to 1.8984375
- w_query2: bfloat16 [1536, 1536], P('wide', 'narrow'), may hold values from -0.15625 to 0.15625
- b_query2: bfloat16 [1536], P('narrow'), may hold values from -3 to 3
- w_keyval2: bfloat16 [1536, 512], P('wide'), may hold values from -0.15625 to 0.15625
- b_keyval2: bfloat16 [512], replicated, may hold values from -3 to 3
Outputs:
- hidden_out: bfloat16 [4096, 1536], P('wide')
- next_query: bfloat16 [4096, 1536], P('wide', 'narrow')
- next_keyval: bfloat16 [4096, 512], P('wide', 'narrow')
- kv_cache: bfloat16 [4, 40, 128, 128], P('narrow', 'wide')
Inputs may be any that keep to these rules, and one draw needn't show every extreme that they name: `segment_ids`: segment s covers tokens seg_offsets[s] to seg_offsets[s] + seg_lengths[s] - 1. `seg_lengths`: they sum to 4096. seg_offsets[0] = 0 and seg_offsets[s + 1] = seg_offsets[s] + seg_lengths[s]. `block_table`: entry j of row s is a page for j below ceil(seg_lengths[s] / 128) and -1 beyond; no page appears twice.
All inputs are finite; a program needn't handle non-finite values.
Results may differ from a plain program's by a relative error of at most 0.017.
Values may be sent and summed in bfloat16 or wider, within the bound.
No kernel may reach another device: no remote copies, remote signals or barrier semaphores. Data moves between devices by JAX's collectives and lax.ppermute only.
A program may use at most 128 MiB of HBM per device.

v0:
```python
import math
import jax
import jax.numpy as jnp
from jax import lax
from jax.sharding import PartitionSpec as P

HD = 128
PAGE_LEN = 128
norm_eps = 1e-06
rope_base = 1000000.0
masked_score = -1e30


def rms_norm(activations, gain_vector):
    values = activations.astype(jnp.float32)
    row_scale = lax.rsqrt(jnp.mean(values * values, axis=-1, keepdims=True) + norm_eps)
    return (values * row_scale * gain_vector.astype(jnp.float32)).astype(jnp.bfloat16)


def rotate(values, positions):
    half_dim = values.shape[-1] // 2
    frequency = rope_base ** (-(jnp.arange(half_dim, dtype=jnp.float32) * 2.0 / values.shape[-1]))
    angles = positions.astype(jnp.float32)[:, None, None] * frequency
    cosine = jnp.cos(angles)
    sine_part = jnp.sin(angles)
    lower_half = values[..., :half_dim]
    upper_half = values[..., half_dim:]
    return jnp.concatenate(
        [
            lower_half * cosine - upper_half * sine_part,
            upper_half * cosine + lower_half * sine_part,
        ],
        axis=-1,
    )


def lookup(table, indices):
    table_match = indices[..., None] == jnp.arange(table.shape[0], dtype=jnp.int32)
    return jnp.sum(jnp.where(table_match, table, 0), axis=-1)


def fold_rows(normed, first_weight, second_weight):
    return (
        jnp.dot(
            normed,
            lax.all_gather(first_weight, "wide", axis=0, tiled=True),
            preferred_element_type=jnp.float32,
        ),
        jnp.dot(
            normed,
            lax.all_gather(second_weight, "wide", axis=0, tiled=True),
            preferred_element_type=jnp.float32,
        ),
    )


def column_terms(left_rows, weight_block):
    return jnp.dot(
        left_rows,
        lax.all_gather(weight_block, "wide", axis=1, tiled=True),
        preferred_element_type=jnp.float32,
    )


def keyval_block(w_keyval, b_keyval, head_pair):
    pair_width = 2 * HD
    pair_offset = head_pair * pair_width
    return (w_keyval, b_keyval, pair_offset)


def add_branch(partial_terms, base_rows, narrow_index):
    share_sum = lax.psum_scatter(
        partial_terms.astype(jnp.bfloat16), "narrow", scatter_dimension=1, tiled=True
    ).astype(jnp.float32)
    share_width = share_sum.shape[1]
    base_share = lax.dynamic_slice_in_dim(base_rows, narrow_index * share_width, share_width, 1)
    updated = (base_share.astype(jnp.float32) + share_sum).astype(jnp.bfloat16)
    result_rows = lax.all_gather(updated, "narrow", axis=1, tiled=True)
    return result_rows


def attend(queries, keys_all, values_all, segment_ids, seg_offsets, row_base):
    tok_rows = queries.shape[0]
    local_heads = queries.shape[1] // HD
    total_rows = keys_all.shape[0]
    key_block = math.gcd(total_rows, 512)
    score_scale = HD ** (-0.5)
    stacked = (
        queries.reshape(tok_rows, local_heads, HD)
        .transpose(1, 0, 2)
        .reshape(local_heads * tok_rows, HD)
    )
    query_pos = row_base + jnp.arange(tok_rows, dtype=jnp.int32)
    query_pos_all = jnp.tile(query_pos, local_heads)
    query_seg_all = jnp.tile(segment_ids, local_heads)
    lowest = lookup(seg_offsets, segment_ids[:1])[0]
    first_block = lowest // key_block
    last_block = (row_base + tok_rows - 1) // key_block

    def visit_block(block_number, state_now):
        running_max, running_sum, accumulated = state_now
        key_start = block_number * key_block
        keys_here = lax.dynamic_slice_in_dim(keys_all, key_start, key_block, 0)
        values_here = lax.dynamic_slice_in_dim(values_all, key_start, key_block, 0)
        key_pos = key_start + jnp.arange(key_block, dtype=jnp.int32)
        key_seg = jnp.sum((key_pos[:, None] >= seg_offsets[None, 1:]).astype(jnp.int32), axis=1)
        visible = (
            (key_seg[None, :] == query_seg_all[:, None])
            & (key_pos[None, :] <= query_pos_all[:, None])
            & (key_pos[None, :] >= 0)
        )
        scores = (
            jnp.einsum("qd,kd->qk", stacked, keys_here, preferred_element_type=jnp.float32)
            * score_scale
        )
        scores = jnp.where(visible, scores, masked_score)
        new_max = jnp.maximum(running_max, jnp.max(scores, axis=1))
        weights = jnp.where(visible, jnp.exp(scores - new_max[:, None]), 0.0)
        factor = jnp.exp(running_max - new_max)
        running_sum = running_sum * factor + jnp.sum(weights, axis=1)
        accumulated = accumulated * factor[:, None] + jnp.dot(
            weights.astype(jnp.bfloat16), values_here, preferred_element_type=jnp.float32
        )
        return (new_max, running_sum, accumulated)

    row_count = stacked.shape[0]
    initial = (
        jnp.full((row_count,), masked_score, jnp.float32),
        jnp.zeros((row_count,), jnp.float32),
        jnp.zeros((row_count, HD), jnp.float32),
    )
    final_max, final_sum, accumulated = lax.fori_loop(
        first_block, last_block + 1, visit_block, initial
    )
    mixed_heads = (
        (accumulated / final_sum[:, None]).reshape(local_heads, tok_rows, HD).transpose(1, 0, 2)
    )
    return mixed_heads.reshape(tok_rows, local_heads * HD).astype(jnp.bfloat16)


def fill_pages(source, seg_lengths, seg_offsets, block_table, first_page, page_count):
    pages_here = first_page + jnp.arange(page_count, dtype=jnp.int32)
    page_match = block_table[None, :, :] == pages_here[:, None, None]
    seg_grid = jnp.arange(block_table.shape[0], dtype=jnp.int32)[None, :, None]
    page_grid = jnp.arange(block_table.shape[1], dtype=jnp.int32)[None, None, :]
    page_owner = jnp.sum(jnp.where(page_match, seg_grid, 0), axis=(1, 2))
    logical = jnp.sum(jnp.where(page_match, page_grid, 0), axis=(1, 2))
    in_use = jnp.any(page_match, axis=(1, 2))
    first_token = lookup(seg_offsets, page_owner) + logical * PAGE_LEN
    filled = lookup(seg_lengths, page_owner) - logical * PAGE_LEN
    slot_index = jnp.arange(PAGE_LEN, dtype=jnp.int32)
    row_ids = jnp.clip(first_token[:, None] + slot_index[None, :], 0, source.shape[0] - 1)
    keep_slot = in_use[:, None] & (slot_index[None, :] < filled[:, None])
    taken_rows = jnp.take(source, row_ids.reshape(-1), axis=0).reshape(
        page_count, PAGE_LEN, source.shape[1]
    )
    return jnp.where(keep_slot[:, :, None], taken_rows, jnp.zeros((), source.dtype))


def local(
    hidden_in,
    segment_ids,
    seg_lengths,
    seg_offsets,
    block_table,
    attn_gain,
    w_query,
    b_query,
    w_keyval,
    b_keyval,
    w_out,
    mlp_gain,
    w_gate,
    w_up,
    w_down,
    next_gain,
    w_query2,
    b_query2,
    w_keyval2,
    b_keyval2,
):
    tok_rows = hidden_in.shape[0]
    wide_index = lax.axis_index("wide")
    narrow_index = lax.axis_index("narrow")
    head_pair = narrow_index // 2
    kind_index = narrow_index % 2
    row_base = wide_index * tok_rows
    positions = row_base + jnp.arange(tok_rows, dtype=jnp.int32) - lookup(seg_offsets, segment_ids)
    normed = rms_norm(hidden_in, attn_gain)
    kv_weight, kv_bias, pair_offset = keyval_block(w_keyval, b_keyval, head_pair)
    query_sum, keyval_sum = fold_rows(normed, w_query, kv_weight)
    queries = query_sum + b_query.astype(jnp.float32)
    local_heads = queries.shape[1] // HD
    queries = (
        rotate(queries.reshape(tok_rows, local_heads, HD), positions)
        .reshape(tok_rows, local_heads * HD)
        .astype(jnp.bfloat16)
    )
    keyvals = (keyval_sum + kv_bias.astype(jnp.float32)).reshape(tok_rows, -1, 2, HD)
    keyvals = jnp.stack([rotate(keyvals[:, :, 0, :], positions), keyvals[:, :, 1, :]], axis=2)
    keyvals = keyvals.reshape(tok_rows, kv_weight.shape[1]).astype(jnp.bfloat16)
    gathered = lax.all_gather(keyvals, "wide", axis=0, tiled=True)
    source = lax.dynamic_slice_in_dim(gathered, pair_offset + kind_index * HD, HD, 1)
    keys_all = lax.dynamic_slice_in_dim(gathered, pair_offset, HD, 1)
    values_all = lax.dynamic_slice_in_dim(gathered, pair_offset + HD, HD, 1)
    mixed_heads = attend(queries, keys_all, values_all, segment_ids, seg_offsets, row_base)
    residual = add_branch(column_terms(mixed_heads, w_out), hidden_in, narrow_index)
    normed_mlp = rms_norm(residual, mlp_gain)
    gate_sum, up_sum = fold_rows(normed_mlp, w_gate, w_up)
    hidden_units = (jax.nn.silu(gate_sum) * up_sum).astype(jnp.bfloat16)
    hidden_out = add_branch(column_terms(hidden_units, w_down), residual, narrow_index)
    normed_next = rms_norm(hidden_out, next_gain)
    kv_weight_next, kv_bias_next, pair_offset_next = keyval_block(w_keyval2, b_keyval2, head_pair)
    query_next, keyval_next = fold_rows(normed_next, w_query2, kv_weight_next)
    next_query = (query_next + b_query2.astype(jnp.float32)).astype(jnp.bfloat16)
    keyval_next = keyval_next + kv_bias_next.astype(jnp.float32)
    next_keyval = lax.dynamic_slice_in_dim(
        keyval_next, pair_offset_next + kind_index * HD, HD, 1
    ).astype(jnp.bfloat16)
    page_count = tok_rows // PAGE_LEN + 1
    cache_block = fill_pages(
        source, seg_lengths, seg_offsets, block_table, wide_index * page_count, page_count
    )
    return (hidden_out, next_query, next_keyval, cache_block[None])


def solution(mesh):
    placed = (
        P("wide", None),
        P("wide"),
        P(),
        P(),
        P(),
        P(),
        P("wide", "narrow"),
        P("narrow"),
        P("wide", None),
        P(),
        P("narrow", "wide"),
        P(),
        P("wide", "narrow"),
        P("wide", "narrow"),
        P("narrow", "wide"),
        P(),
        P("wide", "narrow"),
        P("narrow"),
        P("wide", None),
        P(),
    )
    return jax.shard_map(
        local,
        mesh=mesh,
        in_specs=placed,
        out_specs=(
            P("wide", None),
            P("wide", "narrow"),
            P("wide", "narrow"),
            P("narrow", "wide", None, None),
        ),
        check_vma=False,
    )
```

profile of v0, /device:TPU:0, one launch (start us, length us, event | category | flops | bytes accessed | tf_op | source)
XLA Modules:
  0.0 521.2 jit_solution(14658357420002267087)
XLA Ops:
  7.2 0.7 all-gather.12.cloned.1.call-update
  7.9 0.7 all-gather.16.cloned.1.call-update
  8.7 0.7 convert_element_type.106
  10.1 0.8 select_reduce_fusion
  10.9 1.8 fusion.17
  13.2 25.1 %all-gather.12.cloned.1.call-done = bf16[1536,512]{1,0:T(8,128)(2,1)} async-done(((bf16[192,512]{1,0:T(8,128)(2,1)}), bf16[1536,512]{1,0:T(8,128)(2,1)}) %all-gather.12.cloned.1.call-update) | async-done | bytes 1572880 | tf_op jit(solution)/shard_map/all_gather | solution.py:51
  38.3 3.0 convolution_add_fusion.1
  41.6 1.0 copy.42
  43.8 1.3 fusion.44
  47.8 16.5 %all-gather.16.cloned.1.call-done = bf16[1536,384]{1,0:T(8,128)(2,1)} async-done(((bf16[192,384]{1,0:T(8,128)(2,1)}), bf16[1536,384]{1,0:T(8,128)(2,1)}) %all-gather.16.cloned.1.call-update) | async-done | bytes 1179664 | tf_op jit(solution)/shard_map/all_gather | solution.py:46
  64.3 2.2 convolution_add_fusion.3
  66.9 36.6 %all-gather.14.cloned.1.call-done = bf16[4096,512]{1,0:T(8,128)(2,1)} async-done(((bf16[512,512]{1,0:T(8,128)(2,1)}), bf16[4096,512]{1,0:T(8,128)(2,1)}) %all-gather.14.cloned.1.call-update) | async-done | bytes 4194320 | tf_op jit(solution)/shard_map/all_gather | solution.py:202
  103.5 3.1 constant_dynamic-slice_fusion
  106.6 5.7 %while.15 = (s32[]{:T(128)}, f32[1536]{0:T(1024)S(1)}, f32[1536]{0:T(1024)S(1)}, f32[1536,128]{1,0:T(8,128)S(1)}, s32[]{:T(128)}, /*index=5*/s32[8]{0:T(128)S(1)...) while((s32[]{:T(128)}, f32[1536]{0:T(1024)S(1)}, ...), condition=%wide.region_7.8_spmd.clone, body=%wide.region_3.7_spmd.clone.sunk | while | flops 419576320 | bytes 11870495 | solution.py:132
  106.9 2.2 fusion.73
  109.1 1.4 fusion.74
  110.5 1.8 convolution_add_fusion.5
  112.8 16.5 %all-gather.18.cloned.1.call-done = bf16[384,1536]{0,1:T(8,128)(2,1)} async-done(((bf16[384,192]{0,1:T(8,128)(2,1)}), bf16[384,1536]{0,1:T(8,128)(2,1)}) %all-gather.18.cloned.1.call-update) | async-done | bytes 1179664 | tf_op jit(solution)/shard_map/all_gather | solution.py:60
  129.3 2.3 convolution_convert_fusion.1
  131.6 1.6 copy.43
  133.3 41.8 %reduce-scatter.7.cloned.1.call-done = bf16[384,512]{1,0:T(8,128)(2,1)} async-done(((bf16[1536,512]{1,0:T(8,128)(2,1)}), bf16[384,512]{1,0:T(8,128)(2,1)}) %reduce-scatter.7.cloned.1.call-update) | async-done | bytes 393232
  175.1 1.2 copy.44
  176.3 1.8 add_convert_fusion.1
  178.3 0.7 all-gather.22.cloned.1.call-update
  179.0 0.7 all-gather.24.cloned.1.call-update
  179.8 0.7 all-gather.26.cloned.1.call-update
  180.7 33.7 %all-gather.20.cloned.1.call-done = bf16[512,1536]{1,0:T(8,128)(2,1)} async-done(((bf16[512,384]{1,0:T(8,128)(2,1)}), bf16[512,1536]{1,0:T(8,128)(2,1)}) %all-gather.20.cloned.1.call-update) | async-done | bytes 1572880 | tf_op jit(solution)/shard_map/all_gather | solution.py:78
  214.4 1.8 fusion.20
  216.2 47.9 %all-gather.22.cloned.1.call-done = bf16[1536,2240]{1,0:T(8,128)(2,1)} async-done(((bf16[192,2240]{1,0:T(8,128)(2,1)}), bf16[1536,2240]{1,0:T(8,128)(2,1)}) %all-gather.22.cloned.1.call-update) | async-done | bytes 6881296 | tf_op jit(solution)/shard_map/all_gather | solution.py:46
  264.2 9.5 %fusion.28 = f32[512,2240]{0,1:T(8,128)} fusion(bf16[1536,2240]{1,0:T(8,128)(2,1)} %all-gather.22.cloned.1.call-done, bf16[512,1536]{1,0:T(8,128)(2,1)} %all-gather.20.cloned.1.call-done, f32[1536]{0:T(1024)S(1)} %convert_element_type.121, f32[512]{0:T(512)S(1)} %add_rsqrt_fusion.1), kind=kOutput, calls=%fused_computation.52 | convolution fusion | flops 3526361088 | bytes 13049856 | tf_op jit(solution)/shard_map/dot_general | solution.py:44
  273.6 41.3 %all-gather.24.cloned.1.call-done = bf16[1536,2240]{1,0:T(8,128)(2,1)} async-done(((bf16[192,2240]{1,0:T(8,128)(2,1)}), bf16[1536,2240]{1,0:T(8,128)(2,1)}) %all-gather.24.cloned.1.call-update) | async-done | bytes 6881296 | tf_op jit(solution)/shard_map/all_gather | solution.py:51
  314.9 50.8 %all-gather.26.cloned.1.call-done = bf16[2240,1536]{0,1:T(8,128)(2,1)} async-done(((bf16[2240,192]{0,1:T(8,128)(2,1)}), bf16[2240,1536]{0,1:T(8,128)(2,1)}) %all-gather.26.cloned.1.call-update) | async-done | bytes 6881296 | tf_op jit(solution)/shard_map/all_gather | solution.py:60
  365.7 15.9 %convolution_convert_fusion = bf16[512,1536]{1,0:T(8,128)(2,1)} fusion(bf16[2240,1536]{0,1:T(8,128)(2,1)} %all-gather.26.cloned.1.call-done, bf16[1536,2240]{1,0:T(8,128)(2,1)} %all-gather.24.cloned.1.call-done, f32[512,2240]{0,1:T(8,128)} %fusion.28, bf16[512,1536]{1,0:T(8,128)(2,1)S(1)} %copy-done.2, f32[1536]{0:T(1024)S(1)} %convert_element_type.121, ...), kind=kOutput, calls=%fused_computation.40 | convolution fusion | flops 7057244160 | bytes 21504000 | tf_op jit(solution)/shard_map/dot_general | solution.py:58
  381.6 2.7 copy.45
  384.4 35.4 %reduce-scatter.9.cloned.1.call-done = bf16[384,512]{1,0:T(8,128)(2,1)} async-done(((bf16[1536,512]{1,0:T(8,128)(2,1)}), bf16[384,512]{1,0:T(8,128)(2,1)}) %reduce-scatter.9.cloned.1.call-update) | async-done | bytes 393232
  419.8 1.2 copy.46
  421.0 0.8 add_convert_fusion
  422.5 0.7 all-gather.30.cloned.1.call-update
  424.3 2.0 gather_fusion
  426.3 0.9 select_select_fusion
  427.2 30.9 %all-gather.28.cloned.1.call-done = bf16[512,1536]{1,0:T(8,128)(2,1)} async-done(((bf16[512,384]{1,0:T(8,128)(2,1)}), bf16[512,1536]{1,0:T(8,128)(2,1)}) %all-gather.28.cloned.1.call-update) | async-done | bytes 1572880 | tf_op jit(solution)/shard_map/all_gather | solution.py:78
  458.1 1.8 fusion.23
  459.9 24.6 %all-gather.32.cloned.1.call-done = bf16[1536,512]{1,0:T(8,128)(2,1)} async-done(((bf16[192,512]{1,0:T(8,128)(2,1)}), bf16[1536,512]{1,0:T(8,128)(2,1)}) %all-gather.32.cloned.1.call-update) | async-done | bytes 1572880 | tf_op jit(solution)/shard_map/all_gather | solution.py:51
  484.5 2.9 fusion.30
  487.4 0.7 fusion.35
  488.1 22.4 %all-gather.30.cloned.1.call-done = bf16[1536,384]{1,0:T(8,128)(2,1)} async-done(((bf16[192,384]{1,0:T(8,128)(2,1)}), bf16[1536,384]{1,0:T(8,128)(2,1)}) %all-gather.30.cloned.1.call-update) | async-done | bytes 1179664 | tf_op jit(solution)/shard_map/all_gather | solution.py:46
  510.5 3.0 fusion.26
  513.5 1.1 copy.63
  (91 shorter events, 6.1 us)
Async XLA Ops:
  7.2 31.1 %all-gather.12.cloned.1.call-start = ((), (), s32[]{:S(2)}) async-start(), calls=%async_computation.2 | async-start | bytes 1769472 | tf_op jit(solution)/shard_map/all_gather | solution.py:51
  7.9 56.4 %all-gather.16.cloned.1.call-start = ((), (), s32[]{:S(2)}) async-start(), calls=%async_computation.4 | async-start | bytes 1327104 | tf_op jit(solution)/shard_map/all_gather | solution.py:46
  8.6 94.9 %all-gather.14.cloned.1.call-start = ((), (), s32[]{:S(2)}) async-start(), calls=%async_computation.3 | async-start | bytes 4718592 | tf_op jit(solution)/shard_map/all_gather | solution.py:202
  41.3 2.0 copy-start.3
  41.3 2.5 copy-start.7
  41.3 6.4 %copy-start.8 = (bf16[384]{0:T(512)(128)(2,1)S(1)}, bf16[384]{0:T(512)(128)(2,1)}, u32[]{:S(2)}) copy-start(bf16[384]{0:T(512)(128)(2,1)} %param.29) | copy-start | bytes 2308
  41.3 22.9 %copy-start.1 = (bf16[512,1536]{1,0:T(8,128)(2,1)S(1)}, bf16[512,1536]{1,0:T(8,128)(2,1)}, u32[]{:S(2)}) copy-start(bf16[512,1536]{1,0:T(8,128)(2,1)} %param.22) | copy-start | bytes 4718596
  42.7 86.7 %all-gather.18.cloned.1.call-start = ((), (), s32[]{:S(2)}) async-start(), calls=%async_computation.5 | async-start | bytes 1327104 | tf_op jit(solution)/shard_map/all_gather | solution.py:60
  43.2 131.9 %reduce-scatter.7.cloned.1.call-start = ((), (), s32[]{:S(2)}) async-start(), calls=%async_computation.13 | async-start | bytes 1966080
  133.2 47.5 %copy-start.5 = (bf16[1536]{0:T(1024)(128)(2,1)S(1)}, bf16[1536]{0:T(1024)(128)(2,1)}, u32[]{:S(2)}) copy-start(bf16[1536]{0:T(1024)(128)(2,1)} %param.33) | copy-start | bytes 9220
  133.3 81.2 %all-gather.20.cloned.1.call-start = ((), (), s32[]{:S(2)}) async-start(), calls=%async_computation.6 | async-start | bytes 1966080 | tf_op jit(solution)/shard_map/all_gather | solution.py:78
  178.2 85.9 %all-gather.22.cloned.1.call-start = ((), (), s32[]{:S(2)}) async-start(), calls=%async_computation.7 | async-start | bytes 7962624 | tf_op jit(solution)/shard_map/all_gather | solution.py:46
  179.0 136.0 %all-gather.24.cloned.1.call-start = ((), (), s32[]{:S(2)}) async-start(), calls=%async_computation.8 | async-start | bytes 7962624 | tf_op jit(solution)/shard_map/all_gather | solution.py:51
  179.7 186.0 %all-gather.26.cloned.1.call-start = ((), (), s32[]{:S(2)}) async-start(), calls=%async_computation.9 | async-start | bytes 7962624 | tf_op jit(solution)/shard_map/all_gather | solution.py:60
  180.5 239.3 %reduce-scatter.9.cloned.1.call-start = ((), (), s32[]{:S(2)}) async-start(), calls=%async_computation.14 | async-start | bytes 1966080
  216.2 149.5 %copy-start.2 = (bf16[512,1536]{1,0:T(8,128)(2,1)S(1)}, bf16[512,1536]{1,0:T(8,128)(2,1)}, u32[]{:S(2)}) copy-start(bf16[512,1536]{1,0:T(8,128)(2,1)} %all-gather.20.cloned.1.call-done) | copy-start | bytes 4718596
  381.6 41.6 %copy-start.4 = (s32[8,16]{1,0:T(8,128)S(1)}, s32[8,16]{1,0:T(8,128)}, u32[]{:S(2)}) copy-start(s32[8,16]{1,0:T(8,128)} %param.26) | copy-start | bytes 1540
  381.6 42.0 %copy-start.10 = (s32[8]{0:T(128)S(1)}, s32[8]{0:T(128)}, u32[]{:S(2)}) copy-start(s32[8]{0:T(128)} %param.24) | copy-start | bytes 100
  381.6 42.2 %copy-start.6 = (bf16[1536]{0:T(1024)(128)(2,1)S(1)}, bf16[1536]{0:T(1024)(128)(2,1)}, u32[]{:S(2)}) copy-start(bf16[1536]{0:T(1024)(128)(2,1)} %param.37) | copy-start | bytes 9220
  381.6 42.2 %copy-start.11 = (bf16[512]{0:T(512)(128)(2,1)S(1)}, bf16[512]{0:T(512)(128)(2,1)}, u32[]{:S(2)}) copy-start(bf16[512]{0:T(512)(128)(2,1)} %param.41) | copy-start | bytes 3076
  381.6 42.3 %copy-start.9 = (bf16[384]{0:T(512)(128)(2,1)S(1)}, bf16[384]{0:T(512)(128)(2,1)}, u32[]{:S(2)}) copy-start(bf16[384]{0:T(512)(128)(2,1)} %param.39) | copy-start | bytes 2308
  384.3 73.8 %all-gather.28.cloned.1.call-start = ((), (), s32[]{:S(2)}) async-start(), calls=%async_computation.10 | async-start | bytes 1966080 | tf_op jit(solution)/shard_map/all_gather | solution.py:78
  421.9 62.7 %all-gather.32.cloned.1.call-start = ((), (), s32[]{:S(2)}) async-start(), calls=%async_computation.12 | async-start | bytes 1769472 | tf_op jit(solution)/shard_map/all_gather | solution.py:51
  422.4 88.1 %all-gather.30.cloned.1.call-start = ((), (), s32[]{:S(2)}) async-start(), calls=%async_computation.11 | async-start | bytes 1327104 | tf_op jit(solution)/shard_map/all_gather | solution.py:46
  459.9 50.6 %copy-start = (bf16[512,1536]{1,0:T(8,128)(2,1)S(1)}, bf16[512,1536]{1,0:T(8,128)(2,1)}, u32[]{:S(2)}) copy-start(bf16[512,1536]{1,0:T(8,128)(2,1)} %all-gather.28.cloned.1.call-done) | copy-start | bytes 4718596
Sparse Core Ops, SparseCore 0:
  9.9 28.3 all-gather.11
  40.2 24.0 all-gather.15
  66.8 36.7 all-gather.13
  105.2 24.0 all-gather.17
  133.4 41.7 reduce-scatter.6
  178.3 36.0 all-gather.19
  216.3 47.7 all-gather.21
  266.0 48.8 all-gather.23
  316.8 48.8 all-gather.25
  384.5 35.2 reduce-scatter.8
  422.0 36.0 all-gather.27
  459.8 24.6 all-gather.31
  486.4 24.0 all-gather.29
where the time goes:
time: 522 us; the launch traced here: 521 us
  waiting for transfers between devices  429 us (82%)
  matrix products  42.8 us (8%)
  between operations  16.9 us (3%)
  other arithmetic  16.8 us (3%)
  local copies, waits for them, and re-layouts  15.1 us (3%)
    all_gather x3, waiting for transfers between devices, fold_rows(): lax.all_gather(second_weight, 'wide', axis=0, tiled=True)  91 us
    all_gather x3, waiting for transfers between devices, fold_rows(): lax.all_gather(first_weight, 'wide', axis=0, tiled=True)  86.8 us
    unnamed x15, waiting for transfers between devices  82.5 us
    all_gather x2, waiting for transfers between devices, column_terms(): lax.all_gather(weight_block, 'wide', axis=1, tiled=True)  67.3 us
    all_gather x2, waiting for transfers between devices, add_branch(): result_rows = lax.all_gather(updated, 'narrow', axis=1, tiled=True)  64.6 us
    all_gather x1, waiting for transfers between devices, local(): gathered = lax.all_gather(keyvals, 'wide', axis=0, tiled=True)  36.6 us
    dot_general x2, matrix products, column_terms(): jnp.dot(left_rows, lax.all_gather(weight_block, 'wide', axis=1, tiled=Tru...  18.2 us
    dot_general x3, matrix products, fold_rows(): jnp.dot(normed, lax.all_gather(first_weight, 'wide', axis=0, tiled=True),...  14.7 us
  transfers between devices with their start and end apart: 13, of which 13 were waited for; matrix products, arithmetic and copies ran while one was open for 8% of the time, Pallas kernels for 0%

commit v1 on v0

--- a/solution.py
+++ b/solution.py
@@ -9,6 +9,16 @@
 norm_eps = 1e-06
 rope_base = 1000000.0
 masked_score = -1e30
+
+
+def around_the_ring(x, axis, d):
+    size = lax.axis_size(axis)
+    held, tiles = (x, [x])
+    for _ in range(size - 1):
+        held = lax.ppermute(held, axis, [(i, (i + 1) % size) for i in range(size)])
+        tiles.insert(0, held)
+    line = jnp.concatenate(tiles, axis=d)
+    return jnp.roll(line, (lax.axis_index(axis) + 1) * x.shape[d], axis=d)
 
 
 def rms_norm(activations, gain_vector):
@@ -75,7 +85,7 @@
     share_width = share_sum.shape[1]
     base_share = lax.dynamic_slice_in_dim(base_rows, narrow_index * share_width, share_width, 1)
     updated = (base_share.astype(jnp.float32) + share_sum).astype(jnp.bfloat16)
-    result_rows = lax.all_gather(updated, "narrow", axis=1, tiled=True)
+    result_rows = around_the_ring(updated, "narrow", 1)
     return result_rows
 
 

time: 522 us -> 449 us (0.86)
  waiting for transfers between devices: 429 us -> 343 us
  other arithmetic: 16.8 us -> 22.5 us
    all_gather x2 -> x0, waiting for transfers between devices: 64.6 us -> none  [add_branch(): result_rows = lax.all_gather(updated, 'narrow', axis=1, tiled=True)]
    ppermute x0 -> x6, waiting for transfers between devices: none -> 60.5 us  [around_the_ring(): held = lax.ppermute(held, axis, [(i, (i + 1) % size) for i in range(size)])]
    all_gather x3, waiting for transfers between devices: 86.8 us -> 31.6 us  [fold_rows(): lax.all_gather(first_weight, 'wide', axis=0, tiled=True)]
    all_gather x3, waiting for transfers between devices: 91 us -> 65 us  [fold_rows(): lax.all_gather(second_weight, 'wide', axis=0, tiled=True)]
    unnamed x15 -> x13, waiting for transfers between devices: 82.5 us -> 83.2 us
  transfers between devices with their start and end apart: 13 -> 17, of which waited for: 13 -> 16; matrix products, arithmetic and copies ran while one was open for 8% -> 13% of each run, Pallas kernels for 0% -> 0%
where the time goes in v1:
time: 449 us; the launch traced here: 448 us
  waiting for transfers between devices  343 us (76%)
  matrix products  45.2 us (10%)
  other arithmetic  22.5 us (5%)
  local copies, waits for them, and re-layouts  18.7 us (4%)
  between operations  16.9 us (4%)
    unnamed x13, waiting for transfers between devices  83.2 us
    all_gather x2, waiting for transfers between devices, column_terms(): lax.all_gather(weight_block, 'wide', axis=1, tiled=True)  65.8 us
    all_gather x3, waiting for transfers between devices, fold_rows(): lax.all_gather(second_weight, 'wide', axis=0, tiled=True)  65 us
    ppermute x6, waiting for transfers between devices, around_the_ring(): held = lax.ppermute(held, axis, [(i, (i + 1) % size) for i in range(size)])  60.5 us
    all_gather x1, waiting for transfers between devices, local(): gathered = lax.all_gather(keyvals, 'wide', axis=0, tiled=True)  36.6 us
    all_gather x3, waiting for transfers between devices, fold_rows(): lax.all_gather(first_weight, 'wide', axis=0, tiled=True)  31.6 us
    dot_general x2, matrix products, column_terms(): jnp.dot(left_rows, lax.all_gather(weight_block, 'wide', axis=1, tiled=Tru...  18.3 us
    dot_general x3, matrix products, fold_rows(): jnp.dot(normed, lax.all_gather(first_weight, 'wide', axis=0, tiled=True),...  16.1 us
  transfers between devices with their start and end apart: 17, of which 16 were waited for; matrix products, arithmetic and copies ran while one was open for 13% of the time, Pallas kernels for 0%

profile of v1, /device:TPU:0, one launch (start us, length us, event | category | flops | bytes accessed | tf_op | source)
XLA Modules:
  0.0 447.5 jit_solution(9987532575233637468)
XLA Ops:
  10.1 0.8 select_reduce_fusion
  10.9 1.8 fusion.17
  13.2 25.1 %all-gather.10.cloned.1.call-done = bf16[1536,512]{1,0:T(8,128)(2,1)} async-done(((bf16[192,512]{1,0:T(8,128)(2,1)}), bf16[1536,512]{1,0:T(8,128)(2,1)}) %all-gather.10.cloned.1.call-update) | async-done | bytes 1572880 | tf_op jit(solution)/shard_map/all_gather | solution.py:61
  38.3 3.0 convolution_add_fusion.1
  41.6 1.0 copy.42
  43.8 1.3 fusion.56
  47.8 16.5 %all-gather.14.cloned.1.call-done = bf16[1536,384]{1,0:T(8,128)(2,1)} async-done(((bf16[192,384]{1,0:T(8,128)(2,1)}), bf16[1536,384]{1,0:T(8,128)(2,1)}) %all-gather.14.cloned.1.call-update) | async-done | bytes 1179664 | tf_op jit(solution)/shard_map/all_gather | solution.py:56
  64.3 2.2 convolution_add_fusion.3
  66.9 36.6 %all-gather.12.cloned.1.call-done = bf16[4096,512]{1,0:T(8,128)(2,1)} async-done(((bf16[512,512]{1,0:T(8,128)(2,1)}), bf16[4096,512]{1,0:T(8,128)(2,1)}) %all-gather.12.cloned.1.call-update) | async-done | bytes 4194320 | tf_op jit(solution)/shard_map/all_gather | solution.py:212
  103.5 3.6 constant_dynamic-slice_fusion
  107.2 6.6 %while.15 = (s32[]{:T(128)}, f32[1536]{0:T(1024)S(1)}, f32[1536]{0:T(1024)S(1)}, f32[1536,128]{1,0:T(8,128)S(1)}, s32[]{:T(128)}, /*index=5*/s32[8]{0:T(128)S(1)...) while((s32[]{:T(128)}, f32[1536]{0:T(1024)S(1)}, ...), condition=%wide.region_7.8_spmd.clone, body=%wide.region_3.7_spmd.clone.sunk | while | flops 419576320 | bytes 11862303 | solution.py:142
  107.5 2.2 fusion.78
  109.7 1.4 fusion.79
  111.1 2.7 convolution_add_fusion.5
  114.3 15.0 %all-gather.16.cloned.1.call-done = bf16[384,1536]{0,1:T(8,128)(2,1)} async-done(((bf16[384,192]{0,1:T(8,128)(2,1)}), bf16[384,1536]{0,1:T(8,128)(2,1)}) %all-gather.16.cloned.1.call-update) | async-done | bytes 1179664 | tf_op jit(solution)/shard_map/all_gather | solution.py:70
  129.3 2.3 convolution_convert_fusion.1
  131.6 1.6 copy.43
  135.4 44.9 %reduce-scatter.7.cloned.1.call-done = bf16[384,512]{1,0:T(8,128)(2,1)} async-done(((bf16[1536,512]{1,0:T(8,128)(2,1)}), bf16[384,512]{1,0:T(8,128)(2,1)}) %reduce-scatter.7.cloned.1.call-update) | async-done | bytes 393232
  180.3 1.2 copy.44
  182.0 12.1 %collective-permute-done = bf16[512,384]{1,0:T(8,128)(2,1)S(1)} collective-permute-done((bf16[512,384]{1,0:T(8,128)(2,1)S(1)}, bf16[512,384]{1,0:T(8,128)(2,1)S(1)}, u32[]{:S(2)}, u32[]{:S(2)}) %collective-permute-start) | collective-permute-done | bytes 393248 | tf_op jit(solution)/shard_map/ppermute | solution.py:18
  194.1 0.7 copy-done.2
  194.9 11.6 %collective-permute-done.1 = bf16[512,384]{1,0:T(8,128)(2,1)S(1)} collective-permute-done((bf16[512,384]{1,0:T(8,128)(2,1)S(1)}, bf16[512,384]{1,0:T(8,128)(2,1)S(1)}, u32[]{:S(2)}, u32[]{:S(2)}) %collective-permute-start.1) | collective-permute-done | bytes 393248 | tf_op jit(solution)/shard_map/ppermute | solution.py:18
  206.5 0.7 copy-done.3
  207.2 10.0 %collective-permute-done.2 = bf16[512,384]{1,0:T(8,128)(2,1)} collective-permute-done((bf16[512,384]{1,0:T(8,128)(2,1)S(1)}, bf16[512,384]{1,0:T(8,128)(2,1)}, u32[]{:S(2)}, u32[]{:S(2)}) %collective-permute-start.2) | collective-permute-done | bytes 393248 | tf_op jit(solution)/shard_map/ppermute | solution.py:18
  217.3 2.0 maximum_maximum_fusion
  219.3 1.3 fusion.20
  220.6 9.2 %all-gather.18.cloned.1.call-done = bf16[1536,2240]{1,0:T(8,128)(2,1)} async-done(((bf16[192,2240]{1,0:T(8,128)(2,1)}), bf16[1536,2240]{1,0:T(8,128)(2,1)}) %all-gather.18.cloned.1.call-update) | async-done | bytes 6881296 | tf_op jit(solution)/shard_map/all_gather | solution.py:56
  229.9 10.8 %fusion.40 = f32[512,2240]{0,1:T(8,128)} fusion(bf16[1536,2240]{1,0:T(8,128)(2,1)} %all-gather.18.cloned.1.call-done, f32[1536]{0:T(1024)S(1)} %convert_element_type.121, f32[512]{0:T(512)S(1)} %add_rsqrt_fusion.1, bf16[512,3072]{1,0:T(8,128)(2,1)S(1)} %maximum_maximum_fusion, s32[]{:T(128)S(6)} %select_n.139), kind=kOutput, calls=%fused_computation.72 | convolution fusion | flops 3526361088 | bytes 13051908 | tf_op jit(solution)/shard_map/dot_general | solution.py:54
  240.7 39.9 %all-gather.20.cloned.1.call-done = bf16[1536,2240]{1,0:T(8,128)(2,1)} async-done(((bf16[192,2240]{1,0:T(8,128)(2,1)}), bf16[1536,2240]{1,0:T(8,128)(2,1)}) %all-gather.20.cloned.1.call-update) | async-done | bytes 6881296 | tf_op jit(solution)/shard_map/all_gather | solution.py:61
  280.6 50.8 %all-gather.22.cloned.1.call-done = bf16[2240,1536]{0,1:T(8,128)(2,1)} async-done(((bf16[2240,192]{0,1:T(8,128)(2,1)}), bf16[2240,1536]{0,1:T(8,128)(2,1)}) %all-gather.22.cloned.1.call-update) | async-done | bytes 6881296 | tf_op jit(solution)/shard_map/all_gather | solution.py:70
  331.4 16.0 %convolution_convert_fusion = bf16[512,1536]{1,0:T(8,128)(2,1)} fusion(bf16[2240,1536]{0,1:T(8,128)(2,1)} %all-gather.22.cloned.1.call-done, bf16[1536,2240]{1,0:T(8,128)(2,1)} %all-gather.20.cloned.1.call-done, f32[512,2240]{0,1:T(8,128)} %fusion.40, f32[1536]{0:T(1024)S(1)} %convert_element_type.121, f32[512]{0:T(512)S(1)} %add_rsqrt_fusion.1, ...), kind=kOutput, calls=%fused_computation.49 | convolution fusion | flops 7057244160 | bytes 21506052 | tf_op jit(solution)/shard_map/dot_general | solution.py:68
  347.4 2.6 copy.45
  351.4 0.9 fusion.46
  352.3 33.3 %reduce-scatter.9.cloned.1.call-done = bf16[384,512]{1,0:T(8,128)(2,1)} async-done(((bf16[1536,512]{1,0:T(8,128)(2,1)}), bf16[384,512]{1,0:T(8,128)(2,1)}) %reduce-scatter.9.cloned.1.call-update) | async-done | bytes 393232
  385.5 1.9 copy.46
  387.5 1.2 add_convert_fusion
  389.1 0.9 compare_reduce_fusion
  390.0 0.9 select_reduce_fusion.2
  390.9 10.3 %collective-permute-done.3 = bf16[512,384]{1,0:T(8,128)(2,1)S(1)} collective-permute-done((bf16[512,384]{1,0:T(8,128)(2,1)S(1)}, bf16[512,384]{1,0:T(8,128)(2,1)S(1)}, u32[]{:S(2)}, u32[]{:S(2)}) %collective-permute-start.3) | collective-permute-done | bytes 393248 | tf_op jit(solution)/shard_map/ppermute | solution.py:18
  401.4 11.4 %collective-permute-done.4 = bf16[512,384]{1,0:T(8,128)(2,1)S(1)} collective-permute-done((bf16[512,384]{1,0:T(8,128)(2,1)S(1)}, bf16[512,384]{1,0:T(8,128)(2,1)S(1)}, u32[]{:S(2)}, u32[]{:S(2)}) %collective-permute-start.4) | collective-permute-done | bytes 393248 | tf_op jit(solution)/shard_map/ppermute | solution.py:18
  412.8 0.8 dynamic-slice
  414.3 3.3 gather_fusion
  417.6 0.9 select_select_fusion
  418.5 5.0 %collective-permute-done.5 = bf16[512,384]{1,0:T(8,128)(2,1)S(1)} collective-permute-done((bf16[512,384]{1,0:T(8,128)(2,1)S(1)}, bf16[512,384]{1,0:T(8,128)(2,1)S(1)}, u32[]{:S(2)}, u32[]{:S(2)}) %collective-permute-start.5) | collective-permute-done | bytes 393248 | tf_op jit(solution)/shard_map/ppermute | solution.py:18
  423.5 4.8 %fusion.23 = (f32[512]{0:T(512)S(1)}, bf16[512,1536]{1,0:T(8,128)(2,1)S(1)}) fusion(s32[]{:T(128)S(6)} %select_n.139, bf16[512,384]{1,0:T(8,128)(2,1)S(1)} %add_convert_fusion, bf16[512,384]{1,0:T(8,128)(2,1)S(1)} %collective-permute-done.3, bf16[512,384]{1,0:T(8,128)(2,1)S(1)} %collective-permute-done.4, bf16[512,384]{1,0:T(8,128)(2,1)S(1)} %collective-permute-done.5), kind=kLoop, calls=%fused_computation.37 | loop fusion | flops 14941696 | bytes 3147780 | tf_op jit(solution)/shard_map/reduce_sum | solution.py:26
  428.4 3.0 fusion.34
  432.0 5.9 %all-gather.24.cloned.1.call-done = bf16[1536,384]{1,0:T(8,128)(2,1)} async-done(((bf16[192,384]{1,0:T(8,128)(2,1)}), bf16[1536,384]{1,0:T(8,128)(2,1)}) %all-gather.24.cloned.1.call-update) | async-done | bytes 1179664 | tf_op jit(solution)/shard_map/all_gather | solution.py:56
  438.0 3.0 fusion.33
  (95 shorter events, 11.9 us)
Async XLA Ops:
  7.2 31.1 %all-gather.10.cloned.1.call-start = ((), (), s32[]{:S(2)}) async-start(), calls=%async_computation.2 | async-start | bytes 1769472 | tf_op jit(solution)/shard_map/all_gather | solution.py:61
  7.9 56.4 %all-gather.14.cloned.1.call-start = ((), (), s32[]{:S(2)}) async-start(), calls=%async_computation.4 | async-start | bytes 1327104 | tf_op jit(solution)/shard_map/all_gather | solution.py:56
  8.6 94.9 %all-gather.12.cloned.1.call-start = ((), (), s32[]{:S(2)}) async-start(), calls=%async_computation.3 | async-start | bytes 4718592 | tf_op jit(solution)/shard_map/all_gather | solution.py:212
  41.3 2.0 copy-start.4
  41.3 2.5 copy-start.8
  41.3 6.4 %copy-start.10 = (bf16[384]{0:T(512)(128)(2,1)S(1)}, bf16[384]{0:T(512)(128)(2,1)}, u32[]{:S(2)}) copy-start(bf16[384]{0:T(512)(128)(2,1)} %param.31) | copy-start | bytes 2308
  41.3 22.9 %copy-start = (bf16[512,1536]{1,0:T(8,128)(2,1)S(1)}, bf16[512,1536]{1,0:T(8,128)(2,1)}, u32[]{:S(2)}) copy-start(bf16[512,1536]{1,0:T(8,128)(2,1)} %param.24) | copy-start | bytes 4718596
  42.7 86.7 %all-gather.16.cloned.1.call-start = ((), (), s32[]{:S(2)}) async-start(), calls=%async_computation.5 | async-start | bytes 1327104 | tf_op jit(solution)/shard_map/all_gather | solution.py:70
  43.2 137.0 %reduce-scatter.7.cloned.1.call-start = ((), (), s32[]{:S(2)}) async-start(), calls=%async_computation.11 | async-start | bytes 1966080
  133.2 73.3 %copy-start.6 = (bf16[1536]{0:T(1024)(128)(2,1)S(1)}, bf16[1536]{0:T(1024)(128)(2,1)}, u32[]{:S(2)}) copy-start(bf16[1536]{0:T(1024)(128)(2,1)} %param.35) | copy-start | bytes 9220
  133.2 96.6 %all-gather.18.cloned.1.call-start = ((), (), s32[]{:S(2)}) async-start(), calls=%async_computation.6 | async-start | bytes 7962624 | tf_op jit(solution)/shard_map/all_gather | solution.py:56
  133.8 146.8 %all-gather.20.cloned.1.call-start = ((), (), s32[]{:S(2)}) async-start(), calls=%async_computation.7 | async-start | bytes 7962624 | tf_op jit(solution)/shard_map/all_gather | solution.py:61
  134.6 196.8 %all-gather.22.cloned.1.call-start = ((), (), s32[]{:S(2)}) async-start(), calls=%async_computation.8 | async-start | bytes 7962624 | tf_op jit(solution)/shard_map/all_gather | solution.py:70
  135.3 250.2 %reduce-scatter.9.cloned.1.call-start = ((), (), s32[]{:S(2)}) async-start(), calls=%async_computation.12 | async-start | bytes 1966080
  181.6 12.6 %collective-permute-start = (bf16[512,384]{1,0:T(8,128)(2,1)S(1)}, bf16[512,384]{1,0:T(8,128)(2,1)S(1)}, u32[]{:S(2)}, u32[]{:S(2)}) collective-permute-start(bf16[512,384]{1,0:T(8,128)(2,1)S(1)} %add_convert_fusion.1), channel_id=1, source_target_pairs={{0,1},{1,2},{2,3},{3,0},{4,5},{5,6},{6,7},{7,4},{8,9},{9,10},{10,1... | collective-permute-start | bytes 1179656 | tf_op jit(solution)/shard_map/ppermute | solution.py:18
  194.1 0.7 copy-start.2
  194.9 11.6 %collective-permute-start.1 = (bf16[512,384]{1,0:T(8,128)(2,1)S(1)}, bf16[512,384]{1,0:T(8,128)(2,1)S(1)}, u32[]{:S(2)}, u32[]{:S(2)}) collective-permute-start(bf16[512,384]{1,0:T(8,128)(2,1)S(1)} %collective-permute-done), channel_id=1, source_target_pairs={{0,1},{1,2},{2,3},{3,0},{4,5},{5,6},{6,7},{7,4},{8,9},{9,10},{10,1... | collective-permute-start | bytes 1179656 | tf_op jit(solution)/shard_map/ppermute | solution.py:18
  206.5 0.7 copy-start.3
  206.5 10.8 %collective-permute-start.2 = (bf16[512,384]{1,0:T(8,128)(2,1)S(1)}, bf16[512,384]{1,0:T(8,128)(2,1)}, u32[]{:S(2)}, u32[]{:S(2)}) collective-permute-start(bf16[512,384]{1,0:T(8,128)(2,1)S(1)} %collective-permute-done.1), channel_id=1, source_target_pairs={{0,1},{1,2},{2,3},{3,0},{4,5},{5,6},{6,7},{7,4},{8,9},{9,10},{10,1... | collective-permute-start | bytes 1179656 | tf_op jit(solution)/shard_map/ppermute | solution.py:18
  347.4 4.0 copy-start.5
  347.4 65.4 %copy-start.7 = (bf16[1536]{0:T(1024)(128)(2,1)S(1)}, bf16[1536]{0:T(1024)(128)(2,1)}, u32[]{:S(2)}) copy-start(bf16[1536]{0:T(1024)(128)(2,1)} %param.39) | copy-start | bytes 9220
  350.0 78.3 %all-gather.26.cloned.1.call-start = ((), (), s32[]{:S(2)}) async-start(), calls=%async_computation.10 | async-start | bytes 1769472 | tf_op jit(solution)/shard_map/all_gather | solution.py:61
  350.6 87.3 %all-gather.24.cloned.1.call-start = ((), (), s32[]{:S(2)}) async-start(), calls=%async_computation.9 | async-start | bytes 1327104 | tf_op jit(solution)/shard_map/all_gather | solution.py:56
  351.4 34.2 %copy-start.9 = (s32[5]{0:T(128)}, s32[5]{0:T(128)S(1)}, u32[]{:S(2)}) copy-start(s32[5]{0:T(128)S(1)} %iota_add_fusion.2) | copy-start | bytes 64
  388.7 12.5 %collective-permute-start.3 = (bf16[512,384]{1,0:T(8,128)(2,1)S(1)}, bf16[512,384]{1,0:T(8,128)(2,1)S(1)}, u32[]{:S(2)}, u32[]{:S(2)}) collective-permute-start(bf16[512,384]{1,0:T(8,128)(2,1)S(1)} %add_convert_fusion), channel_id=1, source_target_pairs={{0,1},{1,2},{2,3},{3,0},{4,5},{5,6},{6,7},{7,4},{8,9},{9,10},{10,1... | collective-permute-start | bytes 1179656 | tf_op jit(solution)/shard_map/ppermute | solution.py:18
  401.2 11.6 %collective-permute-start.4 = (bf16[512,384]{1,0:T(8,128)(2,1)S(1)}, bf16[512,384]{1,0:T(8,128)(2,1)S(1)}, u32[]{:S(2)}, u32[]{:S(2)}) collective-permute-start(bf16[512,384]{1,0:T(8,128)(2,1)S(1)} %collective-permute-done.3), channel_id=1, source_target_pairs={{0,1},{1,2},{2,3},{3,0},{4,5},{5,6},{6,7},{7,4},{8,9},{9,10},{10,1... | collective-permute-start | bytes 1179656 | tf_op jit(solution)/shard_map/ppermute | solution.py:18
  412.8 10.7 %collective-permute-start.5 = (bf16[512,384]{1,0:T(8,128)(2,1)S(1)}, bf16[512,384]{1,0:T(8,128)(2,1)S(1)}, u32[]{:S(2)}, u32[]{:S(2)}) collective-permute-start(bf16[512,384]{1,0:T(8,128)(2,1)S(1)} %collective-permute-done.4), channel_id=1, source_target_pairs={{0,1},{1,2},{2,3},{3,0},{4,5},{5,6},{6,7},{7,4},{8,9},{9,10},{10,1... | collective-permute-start | bytes 1179656 | tf_op jit(solution)/shard_map/ppermute | solution.py:18
  428.3 9.6 %copy-start.1 = (bf16[512,1536]{1,0:T(8,128)(2,1)}, bf16[512,1536]{1,0:T(8,128)(2,1)S(1)}, u32[]{:S(2)}) copy-start(bf16[512,1536]{1,0:T(8,128)(2,1)S(1)} %get-tuple-element.123) | copy-start | bytes 4718596
Sparse Core Ops, SparseCore 0:
  9.9 28.3 all-gather.9
  40.2 24.0 all-gather.13
  66.8 36.7 all-gather.11
  105.2 24.0 all-gather.15
  133.4 46.8 reduce-scatter.6
  182.0 47.8 all-gather.17
  231.7 48.8 all-gather.19
  282.5 48.8 all-gather.21
  350.2 35.3 reduce-scatter.8
  387.3 24.6 all-gather.25
  413.9 24.0 all-gather.23
